TPU v7x, 512 devices: a whole 4x8x8 slice. The times are simulated.
512 devices in a mesh: dp: 64 (over y, x, core), tensor: 8 (over z).
Axes of the slice: x: 4, y: 8, z: 8, core: 2. Of those that a mesh axis runs over, the one named last changes fastest.
Arguments:
- hidden_act: bfloat16 [32768, 1408], P('dp', 'tensor'), may hold values from -6 to 6
- cotangent: bfloat16 [32768, 2048], P('dp', 'tensor'), may hold values from -4 to 4
- down_table: bfloat16 [1408, 64, 2048], P('tensor', 'dp'), may hold values from -0.15625 to 0.15625
- expert_ids: int32 [128, 4], P('dp'), may hold values from 0 to 31, as said below
- merge_weights: float32 [128, 4], P('dp'), may hold values from 0.1 to 1
- owner_slot: int32 [32], replicated, may hold values from 0 to 63, as said below
Outputs:
- layer_out: bfloat16 [32768, 2048], P('dp', 'tensor')
- grad_hidden: bfloat16 [32768, 1408], P('dp', 'tensor')
- expert_grad: float32 [1408, 64, 2048], P('tensor', 'dp')
Inputs may be any that keep to these rules, and one draw needn't show every extreme that they name: `expert_ids`: each segment lists 4 different experts; the 2 segments of one index of dp list exactly 6 different experts together. `owner_slot`: different experts have different slots; slot 63 always holds an expert.
All inputs are finite; a program needn't handle non-finite values.
Results may differ from a plain program's by a relative error of at most 0.013.
Values may be sent and summed in bfloat16 or wider, within the bound.
A program may use at most 128 MiB of HBM per device.

v0:
```python
import jax
import jax.numpy as jnp
from jax import lax
from jax.sharding import PartitionSpec as P

E = 32
K = 4
ROW_PARTS = 4
PAD = 4


def two_pieces(values):
    high = lax.reduce_precision(values, 8, 7)
    low = lax.reduce_precision(values - high, 8, 7)
    return (high, low)


def exchange(blocks):
    return lax.all_to_all(blocks, "dp", split_axis=0, concat_axis=0, tiled=True)


def split_panels(panels, count):
    lead, ff_local, width = panels.shape
    cols = count // ROW_PARTS
    view = panels.reshape(lead, ROW_PARTS, ff_local // ROW_PARTS, cols, width // cols)
    return jnp.transpose(view, (1, 3, 0, 2, 4)).reshape(
        count, lead, ff_local // ROW_PARTS, width // cols
    )


def join_panels(chunks):
    count, lead, rows, lanes = chunks.shape
    cols = count // ROW_PARTS
    view = chunks.reshape(ROW_PARTS, cols, lead, rows, lanes)
    return jnp.transpose(view, (2, 0, 3, 1, 4)).reshape(lead, ROW_PARTS * rows, cols * lanes)


def body(hidden_act, cotangent, down_table, expert_ids, merge_weights, owner_slot):
    count = lax.axis_size("dp")
    seg_count = expert_ids.shape[0]
    ff_local, _, width = down_table.shape
    row_count = hidden_act.shape[0]
    seg_len = row_count // seg_count
    rows = ff_local // ROW_PARTS
    lanes = width * ROW_PARTS // count
    listed = seg_count * K
    full_cot = lax.all_gather(cotangent, "tensor", axis=1, tiled=True)
    high, low = two_pieces(merge_weights)
    meta = jnp.concatenate(
        [expert_ids.astype(jnp.float32).reshape(-1), high.reshape(-1), low.reshape(-1)]
    ).astype(jnp.bfloat16)
    meta = jnp.pad(meta[None, :], ((0, PAD - 1), (0, lanes - 3 * listed)))
    table_chunks = split_panels(jnp.transpose(down_table, (1, 0, 2)), count)[:, 0]
    outgoing = jnp.concatenate(
        [table_chunks, jnp.broadcast_to(meta[None], (count, PAD, lanes))], axis=1
    )
    arrived = exchange(outgoing)
    by_slot = arrived[:, :rows]
    meta_all = arrived[:, rows, : 3 * listed].astype(jnp.float32)
    ids_all = meta_all[:, :listed].astype(jnp.int32).reshape(count * seg_count, K)
    high_all = meta_all[:, listed : 2 * listed].reshape(count * seg_count, K)
    low_all = meta_all[:, 2 * listed :].reshape(count * seg_count, K)
    experts = jnp.arange(E, dtype=jnp.int32)
    slots_all = jnp.sum(
        jnp.where(ids_all[:, :, None] == experts, owner_slot[None, None, :], 0), axis=2
    )
    hits = slots_all[:, :, None] == jnp.arange(count, dtype=jnp.int32)
    coef = jnp.concatenate(
        [
            jnp.sum(jnp.where(hits, high_all[:, :, None], 0.0), axis=1),
            jnp.sum(jnp.where(hits, low_all[:, :, None], 0.0), axis=1),
        ],
        axis=0,
    ).astype(jnp.bfloat16)
    halves = jnp.einsum("ms,srl->mrl", coef, by_slot, preferred_element_type=jnp.float32)
    merged_chunks = (halves[: count * seg_count] + halves[count * seg_count :]).astype(jnp.bfloat16)
    merged = join_panels(exchange(merged_chunks.reshape(count, seg_count, rows, lanes)))
    hidden_seg = hidden_act.reshape(seg_count, seg_len, ff_local)
    cot_seg = full_cot.reshape(seg_count, seg_len, width)
    seg_grads = jnp.einsum(
        "stf,std->sfd", hidden_seg, cot_seg, preferred_element_type=jnp.float32
    ).astype(jnp.bfloat16)
    returned = exchange(split_panels(seg_grads, count)).reshape(count * seg_count, rows, lanes)
    partial_rows = jnp.einsum(
        "stf,sfd->std", hidden_seg, merged, preferred_element_type=jnp.float32
    ).reshape(row_count, width)
    layer_out = lax.psum_scatter(
        partial_rows.astype(jnp.bfloat16), "tensor", scatter_dimension=1, tiled=True
    )
    grad_hidden = (
        jnp.einsum("std,sfd->stf", cot_seg, merged, preferred_element_type=jnp.float32)
        .astype(jnp.bfloat16)
        .reshape(row_count, ff_local)
    )
    by_segment = jnp.stack([coef[: count * seg_count], coef[count * seg_count :]], axis=1)
    slot_halves = jnp.einsum(
        "mhs,mrl->hsrl", by_segment, returned, preferred_element_type=jnp.float32
    )
    slot_grads = (slot_halves[0] + slot_halves[1]).astype(jnp.bfloat16)
    own_grad = join_panels(exchange(slot_grads)[:, None])
    expert_grad = jnp.transpose(own_grad, (1, 0, 2)).astype(jnp.float32)
    return (layer_out, grad_hidden, expert_grad)


def solution(mesh):
    placed = (
        P("dp", "tensor"),
        P("dp", "tensor"),
        P("tensor", "dp", None),
        P("dp", None),
        P("dp", None),
        P(),
    )
    return jax.shard_map(
        body,
        mesh=mesh,
        in_specs=placed,
        out_specs=(P("dp", "tensor"), P("dp", "tensor"), P("tensor", "dp", None)),
        check_vma=False,
    )
```

profile of v0, /device:TPU:1, one launch (start us, length us, event | category | flops | bytes accessed | tf_op | source)
XLA Modules:
  0.0 178.1 jit_solution(396525168196531516)
XLA Ops:
  8.8 1.3 copy.65
  10.4 1.0 pad_maximum_fusion
  11.4 11.8 %all-to-all-start = ((bf16[64,48,128]{2,1,0:T(8,128)(2,1)}), bf16[64,48,128]{2,1,0:T(8,128)(2,1)S(1)}, u32[]{:S(2)}, u32[]{:S(2)}) async-start(bf16[64,48,128]{2,1,0:T(8,128)(2,1)} %pad_maximum_fusion), calls=%async_computation | async-start | bytes 1572864 | tf_op jit(solution)/shard_map/all_to_all | solution.py:19
  23.9 22.0 %all-to-all-done = bf16[64,48,128]{2,1,0:T(8,128)(2,1)S(1)} async-done(((bf16[64,48,128]{2,1,0:T(8,128)(2,1)}), bf16[64,48,128]{2,1,0:T(8,128)(2,1)S(1)}, u32[]{:S(2)}, u32[]{:S(2)}) %all-to-all-start) | async-done | bytes 786464 | tf_op jit(solution)/shard_map/all_to_all | solution.py:19
  46.6 0.9 fusion.4
  48.1 2.1 %copy.51 = bf16[64,2,44,128]{3,1,2,0:T(2,128)(2,1)} copy(bf16[64,2,44,128]{3,1,0,2:T(2,128)(2,1)S(1)} %bitcast.66) | data formatting | bytes 2883584 | tf_op jit(solution)/shard_map/reshape | solution.py:77
  50.2 6.4 %all-to-all-start.1 = ((bf16[64,2,44,128]{3,1,2,0:T(2,128)(2,1)}), bf16[64,2,44,128]{3,1,2,0:T(2,128)(2,1)S(1)}, u32[]{:S(2)}, u32[]{:S(2)}) async-start(bf16[64,2,44,128]{3,1,2,0:T(2,128)(2,1)} %copy.51), calls=%async_computation.1 | async-start | bytes 2883584 | tf_op jit(solution)/shard_map/all_to_all | solution.py:19
  56.6 20.5 %all-gather.2.cloned.1.call-done = bf16[512,2048]{1,0:T(8,128)(2,1)} async-done(((bf16[512,256]{1,0:T(8,128)(2,1)}), bf16[512,2048]{1,0:T(8,128)(2,1)}) %all-gather.2.cloned.1.call-update) | async-done | bytes 2097168 | tf_op jit(solution)/shard_map/all_gather | solution.py:47
  77.1 2.1 %convolution_convert_fusion.1 = bf16[2,176,2048]{2,1,0:T(8,128)(2,1)S(1)} fusion(bf16[2,256,2048]{2,1,0:T(8,128)(2,1)} %bitcast.63, bf16[22,2,8,256]{3,2,1,0:T(8,128)(2,1)S(1)} %bitcast.77), kind=kOutput, calls=%fused_computation.3 | convolution fusion | flops 369819648 | bytes 3719168 | tf_op jit(solution)/shard_map/stf,std->sfd/dot_general | solution.py:80
  80.0 2.6 %copy.57 = bf16[64,2,44,128]{3,1,2,0:T(2,128)(2,1)} copy(bf16[64,2,44,128]{3,0,2,1:T(8,128)(2,1)S(1)} %bitcast.71) | data formatting | bytes 2883584 | tf_op jit(solution)/shard_map/reshape | solution.py:26
  82.6 10.3 %all-to-all-done.1 = bf16[64,2,44,128]{3,1,2,0:T(2,128)(2,1)S(1)} async-done(((bf16[64,2,44,128]{3,1,2,0:T(2,128)(2,1)}), bf16[64,2,44,128]{3,1,2,0:T(2,128)(2,1)S(1)}, u32[]{:S(2)}, u32[]{:S(2)}) %all-to-all-start.1) | async-done | bytes 1441824 | tf_op jit(solution)/shard_map/all_to_all | solution.py:19
  92.9 6.3 %all-to-all-start.2 = ((bf16[64,2,44,128]{3,1,2,0:T(2,128)(2,1)}), bf16[64,2,44,128]{3,1,2,0:T(2,128)(2,1)S(1)}, u32[]{:S(2)}, u32[]{:S(2)}) async-start(bf16[64,2,44,128]{3,1,2,0:T(2,128)(2,1)} %copy.57), calls=%async_computation.3 | async-start | bytes 2883584 | tf_op jit(solution)/shard_map/all_to_all | solution.py:19
  99.4 1.3 copy.78
  100.7 2.5 %reshape.114 = bf16[2,176,2048]{2,1,0:T(8,128)(2,1)S(1)} reshape(bf16[2,4,44,16,128]{4,3,2,1,0:T(8,128)(2,1)} %bitcast.72) | data formatting | bytes 2883584 | tf_op jit(solution)/shard_map/reshape | solution.py:35
  103.2 2.1 %convolution_convert_fusion = bf16[2,2048,256]{1,2,0:T(8,128)(2,1)} fusion(bf16[2,176,2048]{2,1,0:T(8,128)(2,1)S(1)} %reshape.114, bf16[22,2,8,256]{3,2,1,0:T(8,128)(2,1)S(1)} %bitcast.78), kind=kOutput, calls=%fused_computation | convolution fusion | flops 370147328 | bytes 3719168 | tf_op jit(solution)/shard_map/stf,sfd->std/dot_general | solution.py:84
  105.3 30.3 %all-to-all-done.2 = bf16[64,2,44,128]{3,1,2,0:T(2,128)(2,1)S(1)} async-done(((bf16[64,2,44,128]{3,1,2,0:T(2,128)(2,1)}), bf16[64,2,44,128]{3,1,2,0:T(2,128)(2,1)S(1)}, u32[]{:S(2)}, u32[]{:S(2)}) %all-to-all-start.2) | async-done | bytes 1441824 | tf_op jit(solution)/shard_map/all_to_all | solution.py:19
  135.6 1.5 copy.58
  137.9 1.4 copy.59
  139.3 6.5 %all-to-all-start.3 = ((bf16[64,44,128]{2,1,0:T(8,128)(2,1)}), bf16[64,44,128]{2,1,0:T(8,128)(2,1)}, u32[]{:S(2)}, u32[]{:S(2)}) async-start(bf16[64,44,128]{2,1,0:T(8,128)(2,1)} %copy.59), calls=%async_computation.4 | async-start | bytes 1572864 | tf_op jit(solution)/shard_map/all_to_all | solution.py:19
  145.8 0.8 fusion.2
  146.6 0.7 copy.64
  147.3 21.1 %all-to-all-done.3 = bf16[64,44,128]{2,1,0:T(8,128)(2,1)} async-done(((bf16[64,44,128]{2,1,0:T(8,128)(2,1)}), bf16[64,44,128]{2,1,0:T(8,128)(2,1)}, u32[]{:S(2)}, u32[]{:S(2)}) %all-to-all-start.3) | async-done | bytes 720928 | tf_op jit(solution)/shard_map/all_to_all | solution.py:19
  168.5 1.3 convert_bitcast_fusion
  169.7 1.5 copy.60
  (34 shorter events, 5.7 us)
Async XLA Ops:
  11.4 35.1 %copy-start.2 = (s32[32]{0:T(128)S(1)}, s32[32]{0:T(128)}, u32[]{:S(2)}) copy-start(s32[32]{0:T(128)} %param.11) | copy-start | bytes 388
  11.4 34.5 %all-to-all-start = ((bf16[64,48,128]{2,1,0:T(8,128)(2,1)}), bf16[64,48,128]{2,1,0:T(8,128)(2,1)S(1)}, u32[]{:S(2)}, u32[]{:S(2)}) async-start(bf16[64,48,128]{2,1,0:T(8,128)(2,1)} %pad_maximum_fusion), calls=%async_computation | async-start | bytes 1572864 | tf_op jit(solution)/shard_map/all_to_all | solution.py:19
  23.1 54.0 %all-gather.2.cloned.1.call-start = ((), (), s32[]{:S(2)}) async-start(), calls=%async_computation.6 | async-start | bytes 2359296 | tf_op jit(solution)/shard_map/all_gather | solution.py:47
  50.2 26.9 %copy-start.1 = (bf16[512,176]{0,1:T(8,128)(2,1)S(1)}, bf16[512,176]{0,1:T(8,128)(2,1)}, u32[]{:S(2)}) copy-start(bf16[512,176]{0,1:T(8,128)(2,1)} %param.6) | copy-start | bytes 540676
  50.2 42.7 %all-to-all-start.1 = ((bf16[64,2,44,128]{3,1,2,0:T(2,128)(2,1)}), bf16[64,2,44,128]{3,1,2,0:T(2,128)(2,1)S(1)}, u32[]{:S(2)}, u32[]{:S(2)}) async-start(bf16[64,2,44,128]{3,1,2,0:T(2,128)(2,1)} %copy.51), calls=%async_computation.1 | async-start | bytes 2883584 | tf_op jit(solution)/shard_map/all_to_all | solution.py:19
  92.9 42.7 %all-to-all-start.2 = ((bf16[64,2,44,128]{3,1,2,0:T(2,128)(2,1)}), bf16[64,2,44,128]{3,1,2,0:T(2,128)(2,1)S(1)}, u32[]{:S(2)}, u32[]{:S(2)}) async-start(bf16[64,2,44,128]{3,1,2,0:T(2,128)(2,1)} %copy.57), calls=%async_computation.3 | async-start | bytes 2883584 | tf_op jit(solution)/shard_map/all_to_all | solution.py:19
  99.2 72.1 %reduce-scatter.2.cloned.1.call-start = ((), (), s32[]{:S(2)}) async-start(), calls=%async_computation.5 | async-start | bytes 2359296 | tf_op jit(solution)/shard_map/reduce_scatter | solution.py:87
  137.9 7.8 %copy-start = (bf16[512,2048]{1,0:T(8,128)(2,1)S(1)}, bf16[512,2048]{1,0:T(8,128)(2,1)}, u32[]{:S(2)}) copy-start(bf16[512,2048]{1,0:T(8,128)(2,1)} %all-gather.2.cloned.1.call-done) | copy-start | bytes 6291460
  139.3 29.2 %all-to-all-start.3 = ((bf16[64,44,128]{2,1,0:T(8,128)(2,1)}), bf16[64,44,128]{2,1,0:T(8,128)(2,1)}, u32[]{:S(2)}, u32[]{:S(2)}) async-start(bf16[64,44,128]{2,1,0:T(8,128)(2,1)} %copy.59), calls=%async_computation.4 | async-start | bytes 1572864 | tf_op jit(solution)/shard_map/all_to_all | solution.py:19
Sparse Core Ops, SparseCore 0:
  26.0 51.0 all-gather.1
  105.4 45.6 reduce-scatter.1
where the time goes:
time: 179 us; the launch traced here: 178 us
  waiting for transfers between devices  105 us (59%)
  starting transfers between devices  31.1 us (17%)
  local copies, waits for them, and re-layouts  16.5 us (9%)
  between operations  14.2 us (8%)
  matrix products  6.5 us (4%)
  other arithmetic  4.78 us (3%)
    all_to_all x4, waiting for transfers between devices, exchange(): return lax.all_to_all(blocks, 'dp', split_axis=0, concat_axis=0, tiled=True)  83.7 us
    all_to_all x4, starting transfers between devices, exchange(): return lax.all_to_all(blocks, 'dp', split_axis=0, concat_axis=0, tiled=True)  30.9 us
    all_gather x1, waiting for transfers between devices, body(): full_cot = lax.all_gather(cotangent, 'tensor', axis=1, tiled=True)  20.5 us
  transfers between devices with their start and end apart: 6, of which 5 were waited for; matrix products, arithmetic and copies ran while one was open for 13% of the time, Pallas kernels for 0%

commit v1 on v0

--- a/solution.py
+++ b/solution.py
@@ -44,7 +44,9 @@
     rows = ff_local // ROW_PARTS
     lanes = width * ROW_PARTS // count
     listed = seg_count * K
-    full_cot = lax.all_gather(cotangent, "tensor", axis=1, tiled=True)
+    full_cot = jnp.concatenate(
+        lax.all_to_all(jnp.stack([cotangent] * lax.axis_size("tensor")), "tensor", 0, 0), axis=1
+    )
     high, low = two_pieces(merge_weights)
     meta = jnp.concatenate(
         [expert_ids.astype(jnp.float32).reshape(-1), high.reshape(-1), low.reshape(-1)]

time: 179 us -> 238 us (1.33)
  blocking collectives: 0 us -> 34.2 us
  waiting for transfers between devices: 105 us -> 121 us
  local copies, waits for them, and re-layouts: 16.5 us -> 24.8 us
    all_to_all x0 -> x1, waiting for transfers between devices: none -> 44.1 us  [body(): lax.all_to_all(jnp.stack([cotangent] * lax.axis_size('tensor')), 'tensor'...]
    all_to_all x0 -> x1, blocking collectives: none -> 34.2 us  [exchange(): return lax.all_to_all(blocks, 'dp', split_axis=0, concat_axis=0, tiled=True)]
    all_gather x1 -> x0, waiting for transfers between devices: 20.5 us -> none  [body(): full_cot = lax.all_gather(cotangent, 'tensor', axis=1, tiled=True)]
    all_to_all x0 -> x1, starting transfers between devices: none -> 10.2 us  [body(): lax.all_to_all(jnp.stack([cotangent] * lax.axis_size('tensor')), 'tensor'...]
    all_to_all x4 -> x3, starting transfers between devices: 30.9 us -> 22 us  [exchange(): return lax.all_to_all(blocks, 'dp', split_axis=0, concat_axis=0, tiled=True)]
    all_to_all x4 -> x3, waiting for transfers between devices: 83.7 us -> 76.5 us  [exchange(): return lax.all_to_all(blocks, 'dp', split_axis=0, concat_axis=0, tiled=True)]
    another operation x0 -> x2, local copies, waits for them, and re-layouts: none -> 4.36 us  [the longest x1 2.87 us: body(): cot_seg = full_cot.reshape(seg_count, seg_len, width)]
    reshape x0 -> x1, local copies, waits for them, and re-layouts: none -> 2.53 us  [body(): jnp.concatenate(lax.all_to_all(jnp.stack([cotangent] * lax.axis_size('ten...]
  transfers between devices with their start and end apart: 6 -> 5, of which waited for: 5 -> 4; matrix products, arithmetic and copies ran while one was open for 13% -> 13% of each run, Pallas kernels for 0% -> 0%
where the time goes in v1:
time: 238 us; the launch traced here: 237 us
  waiting for transfers between devices  121 us (51%)
  blocking collectives  34.2 us (14%)
  starting transfers between devices  32.4 us (14%)
  local copies, waits for them, and re-layouts  24.8 us (10%)
  between operations  14.2 us (6%)
  matrix products  6.81 us (3%)
  other arithmetic  3.9 us (2%)
    all_to_all x3, waiting for transfers between devices, exchange(): return lax.all_to_all(blocks, 'dp', split_axis=0, concat_axis=0, tiled=True)  76.5 us
    all_to_all x1, waiting for transfers between devices, body(): lax.all_to_all(jnp.stack([cotangent] * lax.axis_size('tensor')), 'tensor'...  44.1 us
    all_to_all x1, blocking collectives, exchange(): return lax.all_to_all(blocks, 'dp', split_axis=0, concat_axis=0, tiled=True)  34.2 us
    all_to_all x3, starting transfers between devices, exchange(): return lax.all_to_all(blocks, 'dp', split_axis=0, concat_axis=0, tiled=True)  22 us
    all_to_all x1, starting transfers between devices, body(): lax.all_to_all(jnp.stack([cotangent] * lax.axis_size('tensor')), 'tensor'...  10.2 us
  transfers between devices with their start and end apart: 5, of which 4 were waited for; matrix products, arithmetic and copies ran while one was open for 13% of the time, Pallas kernels for 0%

profile of v1, /device:TPU:1, one launch (start us, length us, event | category | flops | bytes accessed | tf_op | source)
XLA Modules:
  0.0 236.9 jit_solution(8688452059037920195)
XLA Ops:
  8.8 1.3 copy.68
  10.5 34.2 %all_to_all.25 = bf16[64,48,128]{2,1,0:T(8,128)(2,1)S(1)} all-to-all(bf16[64,48,128]{2,1,0:T(8,128)(2,1)S(1)} %pad_maximum_fusion), channel_id=1, replica_groups=mesh['dp'=64,'tensor'=8] {'dp'}, dimensions={0} | all-to-all | bytes 1572864 | tf_op jit(solution)/shard_map/all_to_all | solution.py:19
  44.7 1.5 stack.8
  46.2 10.2 %all-to-all-start.2 = ((bf16[8,512,256]{2,1,0:T(8,128)(2,1)}), bf16[8,512,256]{2,1,0:T(8,128)(2,1)S(1)}, u32[]{:S(2)}, u32[]{:S(2)}) async-start(bf16[8,512,256]{2,1,0:T(8,128)(2,1)} %stack.8), calls=%async_computation.3 | async-start | bytes 4194304 | tf_op jit(solution)/shard_map/all_to_all | solution.py:48
  57.1 0.9 fusion.4
  58.6 2.1 copy.53
  60.7 44.1 %all-to-all-done.2 = bf16[8,512,256]{2,1,0:T(8,128)(2,1)S(1)} async-done(((bf16[8,512,256]{2,1,0:T(8,128)(2,1)}), bf16[8,512,256]{2,1,0:T(8,128)(2,1)S(1)}, u32[]{:S(2)}, u32[]{:S(2)}) %all-to-all-start.2) | async-done | bytes 2097184 | tf_op jit(solution)/shard_map/all_to_all | solution.py:48
  104.7 9.1 %all-to-all-start.1 = ((bf16[64,2,44,128]{3,1,2,0:T(2,128)(2,1)}), bf16[64,2,44,128]{3,1,2,0:T(2,128)(2,1)S(1)}, u32[]{:S(2)}, u32[]{:S(2)}) async-start(bf16[64,2,44,128]{3,1,2,0:T(2,128)(2,1)} %copy.53), calls=%async_computation.1 | async-start | bytes 2883584 | tf_op jit(solution)/shard_map/all_to_all | solution.py:19
  113.8 2.5 %copy.56 = bf16[512,8,256]{2,1,0:T(8,128)(2,1)} copy(bf16[512,8,256]{2,0,1:T(8,128)(2,1)S(1)} %bitcast.64) | data formatting | bytes 4194304 | tf_op jit(solution)/shard_map/reshape | solution.py:47
  116.4 2.9 %reshape_reshape.3 = bf16[2,256,2048]{2,1,0:T(8,128)(2,1)S(1)} reshape(bf16[512,8,256]{2,1,0:T(8,128)(2,1)} %copy.56) | data formatting | bytes 4194304 | tf_op jit(solution)/shard_map/reshape;reshape | solution.py:81
  119.2 1.5 convolution_convert_fusion.1
  121.5 2.6 %copy.60 = bf16[64,2,44,128]{3,1,2,0:T(2,128)(2,1)} copy(bf16[64,2,44,128]{3,0,2,1:T(8,128)(2,1)S(1)} %bitcast.70) | data formatting | bytes 2883584 | tf_op jit(solution)/shard_map/reshape | solution.py:26
  124.1 26.1 %all-to-all-done.1 = bf16[64,2,44,128]{3,1,2,0:T(2,128)(2,1)S(1)} async-done(((bf16[64,2,44,128]{3,1,2,0:T(2,128)(2,1)}), bf16[64,2,44,128]{3,1,2,0:T(2,128)(2,1)S(1)}, u32[]{:S(2)}, u32[]{:S(2)}) %all-to-all-start.1) | async-done | bytes 1441824 | tf_op jit(solution)/shard_map/all_to_all | solution.py:19
  150.2 6.5 %all-to-all-start.3 = ((bf16[64,2,44,128]{3,1,2,0:T(2,128)(2,1)}), bf16[64,2,44,128]{3,1,2,0:T(2,128)(2,1)}, u32[]{:S(2)}, u32[]{:S(2)}) async-start(bf16[64,2,44,128]{3,1,2,0:T(2,128)(2,1)} %copy.60), calls=%async_computation.4 | async-start | bytes 2883584 | tf_op jit(solution)/shard_map/all_to_all | solution.py:19
  156.9 1.3 copy.81
  158.2 2.5 %reshape.116 = bf16[2,176,2048]{2,1,0:T(8,128)(2,1)S(1)} reshape(bf16[2,4,44,16,128]{4,3,2,1,0:T(8,128)(2,1)} %bitcast.71) | data formatting | bytes 2883584 | tf_op jit(solution)/shard_map/reshape | solution.py:35
  160.6 3.0 %convolution_convert_fusion = bf16[2,2048,256]{1,2,0:T(8,128)(2,1)} fusion(bf16[2,176,2048]{2,1,0:T(8,128)(2,1)S(1)} %reshape.116, bf16[22,2,8,256]{3,2,1,0:T(8,128)(2,1)} %bitcast.77), kind=kOutput, calls=%fused_computation | convolution fusion | flops 370147328 | bytes 3719168 | tf_op jit(solution)/shard_map/stf,sfd->std/dot_general | solution.py:86
  163.7 29.3 %all-to-all-done.3 = bf16[64,2,44,128]{3,1,2,0:T(2,128)(2,1)} async-done(((bf16[64,2,44,128]{3,1,2,0:T(2,128)(2,1)}), bf16[64,2,44,128]{3,1,2,0:T(2,128)(2,1)}, u32[]{:S(2)}, u32[]{:S(2)}) %all-to-all-start.3) | async-done | bytes 1441824 | tf_op jit(solution)/shard_map/all_to_all | solution.py:19
  192.9 2.9 %copy.61 = bf16[64,2,44,128]{3,1,0,2:T(2,128)(2,1)S(1)} copy(bf16[64,2,44,128]{3,1,2,0:T(2,128)(2,1)} %all-to-all-done.3) | data formatting | bytes 2883584 | tf_op jit(solution)/shard_map/all_to_all | solution.py:19
  196.7 1.4 copy.62
  198.1 6.4 %all-to-all-start.4 = ((bf16[64,44,128]{2,1,0:T(8,128)(2,1)}), bf16[64,44,128]{2,1,0:T(8,128)(2,1)}, u32[]{:S(2)}, u32[]{:S(2)}) async-start(bf16[64,44,128]{2,1,0:T(8,128)(2,1)} %copy.62), calls=%async_computation.5 | async-start | bytes 1572864 | tf_op jit(solution)/shard_map/all_to_all | solution.py:19
  206.1 21.2 %all-to-all-done.4 = bf16[64,44,128]{2,1,0:T(8,128)(2,1)} async-done(((bf16[64,44,128]{2,1,0:T(8,128)(2,1)}), bf16[64,44,128]{2,1,0:T(8,128)(2,1)}, u32[]{:S(2)}, u32[]{:S(2)}) %all-to-all-start.4) | async-done | bytes 720928 | tf_op jit(solution)/shard_map/all_to_all | solution.py:19
  227.2 1.3 convert_bitcast_fusion
  228.5 1.5 copy.63
  (37 shorter events, 6.6 us)
Async XLA Ops:
  10.4 34.3 %copy-start = (bf16[512,256]{1,0:T(8,128)(2,1)S(1)}, bf16[512,256]{1,0:T(8,128)(2,1)}, u32[]{:S(2)}) copy-start(bf16[512,256]{1,0:T(8,128)(2,1)} %param.7) | copy-start | bytes 786436
  46.2 10.7 %copy-start.3 = (s32[32]{0:T(128)S(1)}, s32[32]{0:T(128)}, u32[]{:S(2)}) copy-start(s32[32]{0:T(128)} %param.11) | copy-start | bytes 388
  46.2 58.6 %all-to-all-start.2 = ((bf16[8,512,256]{2,1,0:T(8,128)(2,1)}), bf16[8,512,256]{2,1,0:T(8,128)(2,1)S(1)}, u32[]{:S(2)}, u32[]{:S(2)}) async-start(bf16[8,512,256]{2,1,0:T(8,128)(2,1)} %stack.8), calls=%async_computation.3 | async-start | bytes 4194304 | tf_op jit(solution)/shard_map/all_to_all | solution.py:48
  57.1 0.9 copy-start.1
  104.7 45.5 %all-to-all-start.1 = ((bf16[64,2,44,128]{3,1,2,0:T(2,128)(2,1)}), bf16[64,2,44,128]{3,1,2,0:T(2,128)(2,1)S(1)}, u32[]{:S(2)}, u32[]{:S(2)}) async-start(bf16[64,2,44,128]{3,1,2,0:T(2,128)(2,1)} %copy.53), calls=%async_computation.1 | async-start | bytes 2883584 | tf_op jit(solution)/shard_map/all_to_all | solution.py:19
  150.2 42.8 %all-to-all-start.3 = ((bf16[64,2,44,128]{3,1,2,0:T(2,128)(2,1)}), bf16[64,2,44,128]{3,1,2,0:T(2,128)(2,1)}, u32[]{:S(2)}, u32[]{:S(2)}) async-start(bf16[64,2,44,128]{3,1,2,0:T(2,128)(2,1)} %copy.60), calls=%async_computation.4 | async-start | bytes 2883584 | tf_op jit(solution)/shard_map/all_to_all | solution.py:19
  156.6 73.4 %reduce-scatter.2.cloned.1.call-start = ((), (), s32[]{:S(2)}) async-start(), calls=%async_computation.6 | async-start | bytes 2359296 | tf_op jit(solution)/shard_map/reduce_scatter | solution.py:89
  192.9 3.0 %copy-start.2 = (bf16[128,64]{0,1:T(8,128)(2,1)S(1)}, bf16[128,64]{0,1:T(8,128)(2,1)}, u32[]{:S(2)}) copy-start(bf16[128,64]{0,1:T(8,128)(2,1)} %copy-done.1) | copy-start | bytes 49156
  198.1 29.1 %all-to-all-start.4 = ((bf16[64,44,128]{2,1,0:T(8,128)(2,1)}), bf16[64,44,128]{2,1,0:T(8,128)(2,1)}, u32[]{:S(2)}, u32[]{:S(2)}) async-start(bf16[64,44,128]{2,1,0:T(8,128)(2,1)} %copy.62), calls=%async_computation.5 | async-start | bytes 1572864 | tf_op jit(solution)/shard_map/all_to_all | solution.py:19
Sparse Core Ops, SparseCore 0:
  163.8 37.3 reduce-scatter.1
